TPU v7x, 256 devices: a whole 4x4x8 slice. The times are simulated.
256 devices in a mesh: dp: 32 (over y, x, core), shard: 8 (over z).
Axes of the slice: x: 4, y: 4, z: 8, core: 2. Of those that a mesh axis runs over, the one named last changes fastest.
Arguments:
- grads: bfloat16 [2, 32, 4096, 4096], P(None, 'dp', 'shard'), may hold values from -0.5 to 0.5
- basis: float32 [2, 4096, 256], P(None, 'shard'), may hold values from -0.375 to 0.375
- weight: float32 [2, 8, 32, 16, 4096], P(None, 'shard', 'dp'), may hold values from -6 to 6
- moment_m: float32 [2, 4096, 256], P(None, 'dp'), may hold values from -6 to 6
- moment_v: float32 [2, 4096, 256], P(None, 'dp'), may hold values from 0.25 to 4
Outputs:
- new_weight: float32 [2, 8, 32, 16, 4096], P(None, 'shard', 'dp')
- new_m: float32 [2, 4096, 256], P(None, 'dp')
- new_v: float32 [2, 4096, 256], P(None, 'dp')
- new_basis: float32 [2, 4096, 256], P(None, 'shard')
All inputs are finite; a program needn't handle non-finite values.
Results may differ from a plain program's by a relative error of at most 0.0036.
Values may be sent and summed in bfloat16 or wider, within the bound.
A program may use at most 64 MiB of HBM per device.

v0:
```python
import jax
import jax.numpy as jnp
from jax import lax
from jax.sharding import PartitionSpec as P

MATS = 2
NS_STEPS = 5


def adam_step(moment_m, moment_v, projected):
    next_m = 0.9 * moment_m + 0.1 * projected
    next_v = 0.999 * moment_v + 0.001 * projected * projected
    update = 2.0 * (next_m / (1.0 - 0.9**10)) / (jnp.sqrt(next_v / (1.0 - 0.999**10)) + 1e-08)
    return (next_m, next_v, update)


def ns_turn(iterate, gram):
    return 1.5 * iterate - 0.5 * jnp.dot(iterate, gram, precision=lax.Precision.HIGHEST)


def shards(grads, basis, weight, moment_m, moment_v):
    group_index = lax.axis_index("dp")
    rows_weight = weight.shape[3]
    weights_out, firsts, seconds, bases = ([], [], [], [])
    for matrix in range(MATS):
        gradient = grads[matrix, 0]
        basis_local = basis[matrix]
        basis_bf = basis_local.astype(jnp.bfloat16)
        partial_sum = lax.psum_scatter(
            lax.dot_general(
                gradient, basis_bf, (((0,), (0,)), ((), ())), preferred_element_type=jnp.float32
            ),
            "dp",
            scatter_dimension=0,
            tiled=True,
        )
        projected = lax.psum(partial_sum, "shard")
        next_m, next_v, update = adam_step(moment_m[matrix], moment_v[matrix], projected)
        full_update = lax.all_gather(update, "dp", axis=0, tiled=True)
        basis_rows = lax.dynamic_slice_in_dim(
            basis_local, group_index * rows_weight, rows_weight, 0
        )
        delta = jnp.dot(basis_rows, full_update.T, precision=lax.Precision.HIGHEST)
        weights_out.append((weight[matrix, 0, 0] - delta).reshape(weight.shape[1:]))
        projected_bf = projected.astype(jnp.bfloat16)
        refresh_part = jnp.dot(
            gradient,
            lax.all_gather(projected_bf, "dp", axis=0, tiled=True),
            preferred_element_type=jnp.float32,
        )
        refresh = lax.psum(refresh_part, "dp")
        total_sq = lax.psum(jnp.sum(refresh * refresh), "shard")
        iterate = refresh / jnp.sqrt(total_sq + 1e-06)
        first_turn = 0
        for step in range(first_turn, NS_STEPS):
            gram = lax.psum(
                jnp.dot(iterate.T, iterate, precision=lax.Precision.HIGHEST).astype(jnp.bfloat16),
                "shard",
            ).astype(jnp.float32)
            iterate = ns_turn(iterate, gram)
        bases.append(iterate)
        firsts.append(next_m)
        seconds.append(next_v)
    return (jnp.stack(weights_out), jnp.stack(firsts), jnp.stack(seconds), jnp.stack(bases))


def solution(mesh):
    placed = (
        P(None, "dp", "shard", None),
        P(None, "shard", None),
        P(None, "shard", "dp", None, None),
        P(None, "dp", None),
        P(None, "dp", None),
    )
    return jax.shard_map(
        shards,
        mesh=mesh,
        in_specs=placed,
        out_specs=(
            P(None, "shard", "dp", None, None),
            P(None, "dp", None),
            P(None, "dp", None),
            P(None, "shard", None),
        ),
        check_vma=False,
    )
```

profile of v0, /device:TPU:1, one launch (start us, length us, event | category | flops | bytes accessed | tf_op | source)
XLA Modules:
  0.0 1018.5 jit_solution(8599303258596466312)
XLA Ops:
  7.2 5.5 fusion.4
  14.0 5.5 fusion.8
  19.6 85.4 %reduce-scatter.5.cloned.1.call-done = f32[128,256]{1,0:T(8,128)} async-done(((f32[4096,256]{1,0:T(8,128)}), f32[128,256]{1,0:T(8,128)}) %reduce-scatter.5.cloned.1.call-update) | async-done | bytes 131088 | tf_op jit(solution)/shard_map/reduce_scatter | solution.py:29
  104.9 93.3 %reduce-scatter.3.cloned.1.call-done = f32[128,256]{1,0:T(8,128)} async-done(((f32[4096,256]{1,0:T(8,128)}), f32[128,256]{1,0:T(8,128)}) %reduce-scatter.3.cloned.1.call-update) | async-done | bytes 131088 | tf_op jit(solution)/shard_map/reduce_scatter | solution.py:29
  198.3 71.4 %all-reduce.18.cloned.1.call-done = (f32[128,256]{1,0:T(8,128)}, f32[128,256]{1,0:T(8,128)}) async-done(((f32[128,256]{1,0:T(8,128)}, f32[128,256]{1,0:T(8,128)}), (f32[128,256]{1,0:T(8,128)}, f32[128,256]{1,0:T(8,128)})) %all-reduce.18.cloned.1.call-update) | async-done | bytes 262160 | tf_op jit(solution)/shard_map/psum | solution.py:37
  269.8 2.0 add_divide_fusion.1
  272.4 52.9 %all-gather.9.cloned.1.call-done = bf16[4096,256]{1,0:T(8,128)(2,1)} async-done(((bf16[128,256]{1,0:T(8,128)(2,1)}), bf16[4096,256]{1,0:T(8,128)(2,1)}) %all-gather.9.cloned.1.call-update) | async-done | bytes 2097168 | tf_op jit(solution)/shard_map/all_gather | solution.py:48
  325.3 4.9 fusion.14
  330.2 46.1 %all-gather.11.cloned.1.call-done = bf16[4096,256]{1,0:T(8,128)(2,1)} async-done(((bf16[128,256]{1,0:T(8,128)(2,1)}), bf16[4096,256]{1,0:T(8,128)(2,1)}) %all-gather.11.cloned.1.call-update) | async-done | bytes 2097168 | tf_op jit(solution)/shard_map/all_gather | solution.py:48
  376.3 4.9 fusion.17
  381.3 114.6 %all-reduce.16.cloned.1.call-done = (f32[512,256]{0,1:T(8,128)}, f32[512,256]{0,1:T(8,128)}) async-done(((f32[512,256]{0,1:T(8,128)}, f32[512,256]{0,1:T(8,128)}), (f32[512,256]{0,1:T(8,128)}, f32[512,256]{0,1:T(8,128)})) %all-reduce.16.cloned.1.call-update) | async-done | bytes 1048592 | tf_op jit(solution)/shard_map/psum | solution.py:51
  495.8 2.0 multiply_reduce_fusion
  497.8 14.3 %all-reduce.1 = (f32[]{:T(128)}, f32[]{:T(128)}) all-reduce(f32[]{:T(128)} %get-tuple-element.36, f32[]{:T(128)} %get-tuple-element.37), channel_id=1, replica_groups=mesh['dp'=32,'shard'=8] {'shard'}, use_global_device_ids=true, to_apply=%region_14.0 | all-reduce | flops 2 | bytes 16 | tf_op jit(solution)/shard_map/psum | solution.py:52
  513.5 2.5 convolution_convert_fusion.4
  516.1 2.5 convolution_convert_fusion.9
  518.6 68.6 %all-reduce.28.cloned.1.call-done = (bf16[256,256]{1,0:T(8,128)(2,1)}, bf16[256,256]{1,0:T(8,128)(2,1)}) async-done(((bf16[256,256]{1,0:T(8,128)(2,1)}, bf16[256,256]{1,0:T(8,128)(2,1)}), (bf16[256,256]{1,0:T(8,128)(2,1)}, bf16[256,256]{1,0:T(8,128)(2,1)})) %all-reduce.28.cloned.1.call-update) | async-done | bytes 262160 | tf_op jit(solution)/shard_map/psum | solution.py:56
  587.2 1.4 fusion.31
  588.6 1.4 fusion.25
  592.8 71.3 %all-reduce.26.cloned.1.call-done = (bf16[256,256]{1,0:T(8,128)(2,1)}, bf16[256,256]{1,0:T(8,128)(2,1)}) async-done(((bf16[256,256]{1,0:T(8,128)(2,1)}, bf16[256,256]{1,0:T(8,128)(2,1)}), (bf16[256,256]{1,0:T(8,128)(2,1)}, bf16[256,256]{1,0:T(8,128)(2,1)})) %all-reduce.26.cloned.1.call-update) | async-done | bytes 262160 | tf_op jit(solution)/shard_map/psum | solution.py:56
  665.6 1.4 fusion.30
  669.6 71.5 %all-reduce.24.cloned.1.call-done = (bf16[256,256]{1,0:T(8,128)(2,1)}, bf16[256,256]{1,0:T(8,128)(2,1)}) async-done(((bf16[256,256]{1,0:T(8,128)(2,1)}, bf16[256,256]{1,0:T(8,128)(2,1)}), (bf16[256,256]{1,0:T(8,128)(2,1)}, bf16[256,256]{1,0:T(8,128)(2,1)})) %all-reduce.24.cloned.1.call-update) | async-done | bytes 262160 | tf_op jit(solution)/shard_map/psum | solution.py:56
  742.5 1.4 fusion.29
  746.5 71.5 %all-reduce.22.cloned.1.call-done = (bf16[256,256]{1,0:T(8,128)(2,1)}, bf16[256,256]{1,0:T(8,128)(2,1)}) async-done(((bf16[256,256]{1,0:T(8,128)(2,1)}, bf16[256,256]{1,0:T(8,128)(2,1)}), (bf16[256,256]{1,0:T(8,128)(2,1)}, bf16[256,256]{1,0:T(8,128)(2,1)})) %all-reduce.22.cloned.1.call-update) | async-done | bytes 262160 | tf_op jit(solution)/shard_map/psum | solution.py:56
  818.0 1.4 fusion.22
  819.4 1.4 fusion.28
  826.8 68.2 %all-reduce.20.cloned.1.call-done = (bf16[256,256]{1,0:T(8,128)(2,1)}, bf16[256,256]{1,0:T(8,128)(2,1)}) async-done(((bf16[256,256]{1,0:T(8,128)(2,1)}, bf16[256,256]{1,0:T(8,128)(2,1)}), (bf16[256,256]{1,0:T(8,128)(2,1)}, bf16[256,256]{1,0:T(8,128)(2,1)})) %all-reduce.20.cloned.1.call-update) | async-done | bytes 262160 | tf_op jit(solution)/shard_map/psum | solution.py:56
  895.0 1.4 fusion.21
  896.4 1.4 fusion.27
  899.2 53.3 %all-gather.5.cloned.1.call-done = f32[4096,256]{1,0:T(8,128)} async-done(((f32[128,256]{1,0:T(8,128)}), f32[4096,256]{1,0:T(8,128)}) %all-gather.5.cloned.1.call-update) | async-done | bytes 4194320 | tf_op jit(solution)/shard_map/all_gather | solution.py:39
  952.4 5.7 fusion.1
  958.1 47.4 %all-gather.7.cloned.1.call-done = f32[4096,256]{1,0:T(8,128)} async-done(((f32[128,256]{1,0:T(8,128)}), f32[4096,256]{1,0:T(8,128)}) %all-gather.7.cloned.1.call-update) | async-done | bytes 4194320 | tf_op jit(solution)/shard_map/all_gather | solution.py:39
  1005.5 5.7 fusion
  (53 shorter events, 21.1 us)
Async XLA Ops:
  7.2 97.8 %reduce-scatter.5.cloned.1.call-start = ((), (), s32[]{:S(2)}) async-start(), calls=%async_computation.4 | async-start | bytes 4325376 | tf_op jit(solution)/shard_map/reduce_scatter | solution.py:29
  12.8 1.2 copy-start
  12.8 185.5 %reduce-scatter.3.cloned.1.call-start = ((), (), s32[]{:S(2)}) async-start(), calls=%async_computation.2 | async-start | bytes 4325376 | tf_op jit(solution)/shard_map/reduce_scatter | solution.py:29
  19.5 250.3 %copy-start.4 = (f32[2,128,256]{2,1,0:T(8,128)S(1)}, f32[2,128,256]{2,1,0:T(8,128)}, u32[]{:S(2)}) copy-start(f32[2,128,256]{2,1,0:T(8,128)} %param.8) | copy-start | bytes 786436
  19.5 250.3 %copy-start.5 = (f32[2,128,256]{2,1,0:T(8,128)S(1)}, f32[2,128,256]{2,1,0:T(8,128)}, u32[]{:S(2)}) copy-start(f32[2,128,256]{2,1,0:T(8,128)} %param.9) | copy-start | bytes 786436
  19.5 250.2 %all-reduce.18.cloned.1.call-start = ((), (), s32[]{:S(2)}) async-start(), calls=%async_computation.9 | async-start | bytes 524288 | tf_op jit(solution)/shard_map/psum | solution.py:37
  198.3 127.0 %all-gather.9.cloned.1.call-start = ((), (), s32[]{:S(2)}) async-start(), calls=%async_computation.6 | async-start | bytes 2162688 | tf_op jit(solution)/shard_map/all_gather | solution.py:48
  271.7 104.5 %all-gather.11.cloned.1.call-start = ((), (), s32[]{:S(2)}) async-start(), calls=%async_computation.7 | async-start | bytes 2162688 | tf_op jit(solution)/shard_map/all_gather | solution.py:48
  272.3 223.5 %all-reduce.16.cloned.1.call-start = ((), (), s32[]{:S(2)}) async-start(), calls=%async_computation.8 | async-start | bytes 2097152 | tf_op jit(solution)/shard_map/psum | solution.py:51
  381.2 206.0 %all-reduce.28.cloned.1.call-start = ((), (), s32[]{:S(2)}) async-start(), calls=%async_computation.14 | async-start | bytes 524288 | tf_op jit(solution)/shard_map/psum | solution.py:56
  495.8 91.4 %copy-start.3 = (f32[512,256]{0,1:T(8,128)S(1)}, f32[512,256]{0,1:T(8,128)}, u32[]{:S(2)}) copy-start(f32[512,256]{0,1:T(8,128)} %get-tuple-element.9) | copy-start | bytes 1572868
  497.8 90.8 %copy-start.2 = (f32[512,256]{0,1:T(8,128)S(1)}, f32[512,256]{0,1:T(8,128)}, u32[]{:S(2)}) copy-start(f32[512,256]{0,1:T(8,128)} %get-tuple-element.8) | copy-start | bytes 1572868
  518.6 145.6 %all-reduce.26.cloned.1.call-start = ((), (), s32[]{:S(2)}) async-start(), calls=%async_computation.13 | async-start | bytes 524288 | tf_op jit(solution)/shard_map/psum | solution.py:56
  592.6 148.5 %all-reduce.24.cloned.1.call-start = ((), (), s32[]{:S(2)}) async-start(), calls=%async_computation.12 | async-start | bytes 524288 | tf_op jit(solution)/shard_map/psum | solution.py:56
  669.5 148.5 %all-reduce.22.cloned.1.call-start = ((), (), s32[]{:S(2)}) async-start(), calls=%async_computation.11 | async-start | bytes 524288 | tf_op jit(solution)/shard_map/psum | solution.py:56
  746.4 148.5 %all-reduce.20.cloned.1.call-start = ((), (), s32[]{:S(2)}) async-start(), calls=%async_computation.10 | async-start | bytes 524288 | tf_op jit(solution)/shard_map/psum | solution.py:56
  823.3 129.1 %all-gather.5.cloned.1.call-start = ((), (), s32[]{:S(2)}) async-start(), calls=%async_computation.3 | async-start | bytes 4325376 | tf_op jit(solution)/shard_map/all_gather | solution.py:39
  823.9 181.6 %all-gather.7.cloned.1.call-start = ((), (), s32[]{:S(2)}) async-start(), calls=%async_computation.5 | async-start | bytes 4325376 | tf_op jit(solution)/shard_map/all_gather | solution.py:39
  825.9 126.5 %copy-start.1 = (f32[2,1,1,16,4096]{4,3,2,1,0:T(8,128)S(1)}, f32[2,1,1,16,4096]{4,3,2,1,0:T(8,128)}, u32[]{:S(2)}) copy-start(f32[2,1,1,16,4096]{4,3,2,1,0:T(8,128)} %param.7) | copy-start | bytes 1572868
Sparse Core Ops, SparseCore 0:
  12.9 91.9 reduce-scatter.4
  108.9 89.3 reduce-scatter.2
  200.6 69.0 all-reduce.17
  272.7 52.5 all-gather.8
  328.3 47.9 all-gather.10
  381.3 114.4 all-reduce.15
  518.7 68.4 all-reduce.27
  592.7 71.3 all-reduce.25
  669.6 71.3 all-reduce.23
  746.5 71.3 all-reduce.21
  823.5 71.4 all-reduce.19
  897.4 54.9 all-gather.4
  955.0 50.4 all-gather.6
where the time goes:
time: 1020 us
  waiting for transfers between devices  917 us (90%)
  matrix products  61.3 us (6%)
  between operations  15.4 us (2%)
  blocking collectives  14.3 us (1%)
    psum x5, waiting for transfers between devices, shards(): lax.psum(jnp.dot(iterate.T, iterate, precision=lax.Precision.HIGHEST).ast...  351 us
    reduce_scatter x2, waiting for transfers between devices, shards(): lax.psum_scatter(lax.dot_general(gradient, basis_bf, (((0,), (0,)), ((),...  179 us
    psum x1, waiting for transfers between devices, shards(): refresh = lax.psum(refresh_part, 'dp')  115 us
    all_gather x2, waiting for transfers between devices, shards(): full_update = lax.all_gather(update, 'dp', axis=0, tiled=True)  101 us
    all_gather x2, waiting for transfers between devices, shards(): lax.all_gather(projected_bf, 'dp', axis=0, tiled=True)  99 us
    psum x1, waiting for transfers between devices, shards(): projected = lax.psum(partial_sum, 'shard')  71.4 us
  transfers between devices with their start and end apart: 13, of which 13 were waited for; matrix products, arithmetic and copies ran while one was open for 2% of the time, Pallas kernels for 0%

commit v1 on v0

v1 whole, which is shorter than its diff:
```python
import jax
import jax.numpy as jnp
from jax import lax
from jax.experimental import pallas as pl
from jax.experimental.pallas import tpu as pltpu
from jax.sharding import PartitionSpec as P

MESH = pl.DeviceIdType.MESH
NX, NY, NZ = 4, 4, 8
NS_STEPS = 5
F32, BF16 = jnp.float32, jnp.bfloat16
N_SEMS = 160

NN = (((1,), (0,)), ((), ()))
NT = (((1,), (1,)), ((), ()))
TN = (((0,), (0,)), ((), ()))


def split(a):
    hi = a.astype(BF16)
    return hi, (a - hi.astype(F32)).astype(BF16)


def dot3(a, b, dims=NN):
    ah, al = a
    bh, bl = b

    def d(p, q):
        return lax.dot_general(p, q, dims, preferred_element_type=F32)

    return d(ah, bh) + (d(ah, bl) + d(al, bh))


def kernel(
    grads, basis, weight, mom_m, mom_v,
    w_out, m_out, v_out, b_out,
    gbuf, bas, wbuf, mbuf, vbuf, mo, vo,
    pf, pbf, r1, acc, r2, p2, r3, pblk, pfull,
    rpart, q1, qacc, q2, rfull, spart, s3, sfull,
    dlt, d1, d2, d3, xbuf,
    lsem, ssem, rsem,
):
    dp = lax.axis_index("dp")
    z = lax.axis_index("shard")
    c = lax.rem(dp, 2)
    chip = lax.div(dp, 2)
    x = lax.rem(chip, NX)
    y = lax.div(chip, NX)
    other = 1 - c

    def at(yy, xx, cc, zz):
        return ((yy * NX + xx) * 2 + cc, zz)

    partner = at(y, x, other, z)
    xs = [lax.rem(x + d, NX) for d in range(NX)]
    ys = [lax.rem(y + d, NY) for d in range(NY)]
    zs = [lax.rem(z + d, NZ) for d in range(NZ)]
    xdev = [at(y, xs[d], c, z) for d in range(NX)]
    ydev = [at(ys[d], x, c, z) for d in range(NY)]
    zdev = [at(y, x, c, zs[d]) for d in range(NZ)]

    used = [0]

    def take(n=1):
        base = used[0]
        used[0] += n
        return base

    def rcopy(src, dst, device, index):
        return pltpu.make_async_remote_copy(
            src_ref=src, dst_ref=dst, send_sem=ssem.at[index], recv_sem=rsem.at[index],
            device_id=device, device_id_type=MESH,
        )

    pending = []

    def send(src, dst, device):
        copy = rcopy(src, dst, device, take())
        copy.start()
        pending.append(copy)
        return copy

    def recv(copies):
        for copy in copies:
            copy.wait_recv()

    local = [0]

    def load(src, dst):
        copy = pltpu.make_async_copy(src, dst, lsem.at[local[0]])
        local[0] += 1
        copy.start()
        return copy

    l_grad = load(grads.at[c, 0], gbuf.at[0])
    l_bas = load(basis.at[c], bas)
    l_m = load(mom_m.at[c], mbuf.at[c])
    l_v = load(mom_v.at[c], vbuf.at[c])
    l_w = load(weight.at[:, 0, 0], wbuf)

    barrier = pltpu.get_barrier_semaphore()
    peers = [partner] + xdev[1:] + ydev[1:] + zdev[1:]
    for peer in peers:
        pl.semaphore_signal(barrier, inc=1, device_id=peer, device_id_type=MESH)
    pl.semaphore_wait(barrier, len(peers))

    order = [1, 2, 3, 0]
    g_copies = {}
    for dy in order:
        cols = pl.ds(pl.multiple_of(ys[dy] * 1024, 1024), 1024)
        g_copies[dy] = send(grads.at[other, 0, :, cols], gbuf.at[1, :, cols], partner)
    m_copy = send(mom_m.at[other], mbuf.at[c], partner)
    v_copy = send(mom_v.at[other], vbuf.at[c], partner)

    l_bas.wait()
    bas_bf = bas[...].astype(BF16)
    l_grad.wait()

    def block_of(i, yy, xx):
        cols = pl.ds(pl.multiple_of((yy * NX + xx) * 256, 256), 256)
        return lax.dot_general(
            gbuf[i, :, cols], bas_bf, TN, preferred_element_type=F32
        ).reshape(2, 128, 256)

    @pl.loop(0, NX * NY)
    def _(b):
        yy, xx = lax.div(b, NX), lax.rem(b, NX)
        pf[yy, xx] = block_of(0, yy, xx)

    s0 = take(12)
    s1 = take(12)

    def first0(dy, dx):
        xx = lax.rem(x + dx, NX)
        return rcopy(
            pbf.at[ys[dy], xx, 0], r1.at[0, dx - 1, ys[dy]], at(y, xx, c, z), s0 + dy * 3 + dx - 1
        )

    def first1(dy, dx):
        xx = lax.rem(x + dx, NX)
        return rcopy(
            pbf.at[ys[dy], xx, 1], r1.at[1, dy - 1, xx], ydev[dy], s1 + (dy - 1) * 4 + dx
        )

    for dy in order:
        g_copies[dy].wait_recv()

        @pl.loop(1, NX + 1)
        def _(step):
            dx = lax.rem(step, NX)
            xx = lax.rem(x + dx, NX)
            yy = ys[dy]
            value = pf[yy, xx] + block_of(1, yy, xx)
            pf[yy, xx] = value
            pbf[yy, xx] = value.astype(BF16)

            @pl.when(step < NX)
            def _():
                first0(dy, dx).start()

            if dy:
                first1(dy, dx).start()

    second0, second1 = {}, {}
    for d in order:
        for e in range(1, NX):
            first0(d, e).wait_recv()
        total = pf[ys[d], x, 0]
        for e in range(NX - 1):
            total += r1[0, e, ys[d]].astype(F32)
        acc[0, d] = total
        if d:
            second0[d] = send(acc.at[0, d], r2.at[0, d - 1], ydev[d])
        for e in range(1, NY):
            first1(e, d).wait_recv()
        total = pf[y, xs[d], 1]
        for e in range(NY - 1):
            total += r1[1, e, xs[d]].astype(F32)
        acc[1, d] = total
        if d:
            second1[d] = send(acc.at[1, d], r2.at[1, d - 1], xdev[d])

    third = {}
    for h, copies in ((0, second0), (1, second1)):
        recv(copies.values())
        p2[h] = (acc[h, 0] + r2[h, 0] + (r2[h, 1] + r2[h, 2])).reshape(4, 32, 256)
    p2v = p2
    for d in range(1, NZ):
        zz = zs[d]
        third[d] = send(p2v.at[lax.div(zz, 4), lax.rem(zz, 4)], r3.at[d - 1], zdev[d])
    recv(third.values())
    zh, zl = lax.div(z, 4), lax.rem(z, 4)
    total = p2v[zh, zl]
    for d in range(1, NZ):
        total += r3[d - 1]
    pblk[z] = total
    pfull[y, x, zh, zl] = total.astype(BF16)

    z_bf = [send(pfull.at[y, x, zh, zl], pfull.at[y, x, zh, zl], zdev[d]) for d in range(1, NZ)]
    z_f = [send(pblk.at[z], pblk.at[z], zdev[d]) for d in range(1, NZ)]
    recv(z_bf)

    def gather_first(full):
        a = [send(full.at[y, x, 0], full.at[y, x, 0], ydev[d]) for d in range(1, NY)]
        b = [send(full.at[y, x, 1], full.at[y, x, 1], xdev[d]) for d in range(1, NX)]
        return a + b

    def gather_second(full):
        a = [send(full.at[:, x, 0], full.at[:, x, 0], xdev[d]) for d in range(1, NX)]
        b = [send(full.at[y, :, 1], full.at[y, :, 1], ydev[d]) for d in range(1, NY)]
        return a + b

    copies = gather_first(pfull)

    recv(z_f)
    l_m.wait()
    l_v.wait()
    m_copy.wait_recv()
    v_copy.wait_recv()
    proj = pblk[...].reshape(256, 256)
    next_m = 0.9 * mbuf[...].reshape(256, 256) + 0.1 * proj
    next_v = 0.999 * vbuf[...].reshape(256, 256) + 0.001 * proj * proj
    mo[...] = next_m.reshape(2, 128, 256)
    vo[...] = next_v.reshape(2, 128, 256)
    update = 2.0 * (next_m / (1.0 - 0.9**10)) / (jnp.sqrt(next_v / (1.0 - 0.999**10)) + 1e-08)

    recv(copies)
    copies = gather_second(pfull)
    out_local = [load(mo.at[c], m_out.at[c]), load(vo.at[c], v_out.at[c])]
    out_remote = [send(mo.at[other], m_out.at[c], partner), send(vo.at[other], v_out.at[c], partner)]
    up = split(update)
    for i in range(4):
        rows = pl.ds(i * 128, 128)
        dlt[i] = dot3(split(bas[rows]), up, NT).reshape(4, 2, 16, 256)
    d1[x] = dlt[:, x].reshape(4, 2, 16, 256)
    recv(copies)

    x_copies = [send(dlt.at[:, xs[d]], d1.at[x], xdev[d]) for d in range(1, NX)]

    for yy in range(NY):
        cols = pl.ds(yy * 1024, 1024)
        right = pfull[yy].reshape(1024, 256)
        for i in range(2):
            part = jnp.dot(gbuf[i, :, cols], right, preferred_element_type=F32)
            part = part.reshape(4, 4, 2, 16, 256)
            if yy == 0 and i == 0:
                rpart[...] = part
            else:
                rpart[...] += part

    def reduce_first():
        a = {d: send(rpart.at[:, xs[d], 0], q1.at[0, d - 1], xdev[d]) for d in range(1, NX)}
        b = {d: send(rpart.at[ys[d], :, 1], q1.at[1, d - 1], ydev[d]) for d in range(1, NY)}
        return a, b

    a, b = reduce_first()
    recv(x_copies)
    d2[y] = d1[:, y]
    recv(a.values())
    qacc[0] = rpart[:, x, 0] + q1[0, 0] + (q1[0, 1] + q1[0, 2])
    a2 = [send(qacc.at[0, ys[d]], q2.at[0, d - 1], ydev[d]) for d in range(1, NY)]
    recv(b.values())
    qacc[1] = rpart[y, :, 1] + q1[1, 0] + (q1[1, 1] + q1[1, 2])
    b2 = [send(qacc.at[1, xs[d]], q2.at[1, d - 1], xdev[d]) for d in range(1, NX)]
    y_copies = [send(d1.at[:, ys[d]], d2.at[y], ydev[d]) for d in range(1, NY)]
    recv(a2)
    rfull[y, x, 0] = qacc[0, y] + q2[0, 0] + (q2[0, 1] + q2[0, 2])
    recv(b2)
    rfull[y, x, 1] = qacc[1, x] + q2[1, 0] + (q2[1, 1] + q2[1, 2])
    copies = gather_first(rfull)
    recv(copies)
    copies = gather_second(rfull)
    recv(y_copies)
    w_copy = send(d2.at[:, :, other], d3, partner)
    recv(copies)

    rsplit = split(rfull[...].reshape(512, 256))
    spart[...] = dot3(rsplit, rsplit, TN).reshape(4, 4, 2, 8, 256)
    s_copies = [send(spart.at[y, x], s3.at[d - 1], zdev[d]) for d in range(1, NZ)]

    l_w.wait()
    w_copy.wait_recv()
    for b16 in range(16):
        yy, xx = b16 // 4, b16 % 4
        cols = pl.ds(b16 * 256, 256)
        wbuf[c, :, cols] = wbuf[c, :, cols] - d2[yy, xx, c]
        wbuf[other, :, cols] = wbuf[other, :, cols] - d3[yy, xx]
    out_local.append(load(wbuf, w_out.at[:, 0, 0]))

    recv(s_copies)
    total = spart[y, x]
    for d in range(1, NZ):
        total += s3[d - 1]
    sfull[y, x] = total
    copies = gather_first(sfull)
    recv(copies)
    copies = gather_second(sfull)
    recv(copies)

    gram = sfull[...].reshape(256, 256)
    eye = lax.broadcasted_iota(jnp.int32, (256, 256), 0) == lax.broadcasted_iota(jnp.int32, (256, 256), 1)
    total_sq = jnp.sum(jnp.where(eye, gram, 0.0), keepdims=True) + 1e-06
    gram = gram / total_sq
    diag = jnp.where(eye, 1.5, 0.0)
    factor = diag - 0.5 * gram
    poly = factor
    for _ in range(1, NS_STEPS):
        fs = split(factor)
        gram = dot3(split(dot3(split(gram), fs)), fs)
        factor = diag - 0.5 * gram
        poly = dot3(split(poly), split(factor))
    poly = split(poly * lax.rsqrt(total_sq))
    xbuf[...] = dot3(split(rfull[...].reshape(512, 256)), poly)
    out_local.append(load(xbuf, b_out.at[c]))
    out_remote.append(send(xbuf, b_out.at[c], partner))

    recv(out_remote)
    for copy in out_local:
        copy.wait()
    for copy in pending:
        copy.wait_send()
    for dy in range(NY):
        for dx in range(NX):
            if dx:
                first0(dy, dx).wait_send()
            if dy:
                first1(dy, dx).wait_send()


def shards(grads, basis, weight, moment_m, moment_v):
    hbm = pl.BlockSpec(memory_space=pl.ANY)
    V = pltpu.VMEM
    return tuple(
        pl.pallas_call(
            kernel,
            out_shape=(
                jax.ShapeDtypeStruct(weight.shape, F32),
                jax.ShapeDtypeStruct(moment_m.shape, F32),
                jax.ShapeDtypeStruct(moment_v.shape, F32),
                jax.ShapeDtypeStruct(basis.shape, F32),
            ),
            in_specs=[hbm] * 5,
            out_specs=(hbm,) * 4,
            scratch_shapes=[
                V((2, 512, 4096), BF16),
                V((512, 256), F32),
                V((2, 16, 4096), F32),
                V((2, 128, 256), F32),
                V((2, 128, 256), F32),
                V((2, 128, 256), F32),
                V((2, 128, 256), F32),
                V((4, 4, 2, 128, 256), F32),
                V((4, 4, 2, 128, 256), BF16),
                V((2, 3, 4, 128, 256), BF16),
                V((2, 4, 128, 256), F32),
                V((2, 3, 128, 256), F32),
                V((2, 4, 32, 256), F32),
                V((7, 32, 256), F32),
                V((8, 32, 256), F32),
                V((4, 4, 2, 4, 32, 256), BF16),
                V((4, 4, 2, 16, 256), F32),
                V((2, 3, 4, 16, 256), F32),
                V((2, 4, 16, 256), F32),
                V((2, 3, 16, 256), F32),
                V((4, 4, 2, 16, 256), F32),
                V((4, 4, 2, 8, 256), F32),
                V((7, 2, 8, 256), F32),
                V((4, 4, 2, 8, 256), F32),
                V((4, 4, 2, 16, 256), F32),
                V((4, 4, 2, 16, 256), F32),
                V((4, 4, 2, 16, 256), F32),
                V((4, 4, 16, 256), F32),
                V((512, 256), F32),
                pltpu.SemaphoreType.DMA((12,)),
                pltpu.SemaphoreType.DMA((N_SEMS,)),
                pltpu.SemaphoreType.DMA((N_SEMS,)),
            ],
            compiler_params=pltpu.CompilerParams(
                collective_id=0, has_side_effects=True, vmem_limit_bytes=60 * 1024 * 1024
            ),
        )(grads, basis, weight, moment_m, moment_v)
    )


def solution(mesh):
    placed = (
        P(None, "dp", "shard", None),
        P(None, "shard", None),
        P(None, "shard", "dp", None, None),
        P(None, "dp", None),
        P(None, "dp", None),
    )
    return jax.shard_map(
        shards,
        mesh=mesh,
        in_specs=placed,
        out_specs=(
            P(None, "shard", "dp", None, None),
            P(None, "dp", None),
            P(None, "dp", None),
            P(None, "shard", None),
        ),
        check_vma=False,
    )
```

time: 1020 us -> 122 us (0.12)
  waiting for transfers between devices: 917 us -> 0 us
  Pallas kernels: 0 us -> 113 us
  matrix products: 61.3 us -> 0 us
  between operations: 15.4 us -> 0.64 us
  blocking collectives: 14.3 us -> 0 us
    psum x7 -> x0, waiting for transfers between devices: 537 us -> none  [the longest x5 351 us: shards(): lax.psum(jnp.dot(iterate.T, iterate, precision=lax.Precision.HIGHEST).ast...]
    all_gather x4 -> x0, waiting for transfers between devices: 200 us -> none  [the longest x2 101 us: shards(): full_update = lax.all_gather(update, 'dp', axis=0, tiled=True)]
    reduce_scatter x2 -> x0, waiting for transfers between devices: 179 us -> none  [shards(): lax.psum_scatter(lax.dot_general(gradient, basis_bf, (((0,), (0,)), ((),...]
    pallas_call x0 -> x1, Pallas kernels: none -> 113 us  [shards(): pl.pallas_call(kernel, out_shape=(jax.ShapeDtypeStruct(weight.shape, F32)...]
    dot_general x26 -> x0, matrix products: 61.3 us -> none  [the longest x10 15.2 us: shards(): jnp.dot(iterate.T, iterate, precision=lax.Precision.HIGHEST)]
    psum x1 -> x0, blocking collectives: 14.3 us -> none  [shards(): total_sq = lax.psum(jnp.sum(refresh * refresh), 'shard')]
  transfers between devices with their start and end apart: 13 -> 0, of which waited for: 13 -> 0; matrix products, arithmetic and copies ran while one was open for 2% -> 0% of each run, Pallas kernels for 0% -> 0%
where the time goes in v1:
time: 122 us
  Pallas kernels  113 us (93%)
  local copies, waits for them, and re-layouts  7.47 us (6%)
    pallas_call x1, Pallas kernels, shards(): pl.pallas_call(kernel, out_shape=(jax.ShapeDtypeStruct(weight.shape, F32)...  113 us
    unnamed x4, local copies, waits for them, and re-layouts  7.47 us

profile of v1, /device:TPU:1, one launch (start us, length us, event | category | flops | bytes accessed | tf_op | source)
XLA Modules:
  0.0 121.6 jit_solution(10542894656352474221)
XLA Ops:
  0.6 113.5 %shard_map.84 = (f32[2,1,1,16,4096]{4,3,2,1,0:T(8,128)}, f32[2,128,256]{2,1,0:T(8,128)}, f32[2,128,256]{2,1,0:T(8,128)}, f32[2,512,256]{2,1,0:T(8,128)}) custom-call(bf16[2,1,512,4096]{3,2,1,0:T(8,128)(2,1)} %grads.1, f32[2,512,256]{2,1,0:T(8,128)} %basis.1, f32[2,1,1,16,4096]{4,3,2,1,0:T(8,128)} %weight.1, f32[2,128,256]{2,1,0:T(8,128)} %mom_m.1, ...), custom_call_target="tpu_custom_call" | custom-call | tf_op jit(solution)/shard_map/pallas_call | solution.py:334
  114.1 1.9 %copy.13 = f32[2,1,1,16,4096]{4,3,2,1,0:T(8,128)} copy(f32[2,1,1,16,4096]{4,3,2,1,0:T(8,128)} %get-tuple-element.8) | data formatting | bytes 1048576
  116.0 1.7 %copy.14 = f32[2,128,256]{2,1,0:T(8,128)} copy(f32[2,128,256]{2,1,0:T(8,128)} %get-tuple-element.9) | data formatting | bytes 524288
  117.6 1.7 %copy.15 = f32[2,128,256]{2,1,0:T(8,128)} copy(f32[2,128,256]{2,1,0:T(8,128)} %get-tuple-element.10) | data formatting | bytes 524288
  119.3 2.3 %copy.16 = f32[2,512,256]{2,1,0:T(8,128)} copy(f32[2,512,256]{2,1,0:T(8,128)} %get-tuple-element.11) | data formatting | bytes 2097152
